TPU v7x, 32 devices: a whole 2x2x4 slice. The times are simulated.
32 devices in a mesh: row: 8 (over y, x, core), col: 4 (over z).
Axes of the slice: x: 2, y: 2, z: 4, core: 2. Of those that a mesh axis runs over, the one named last changes fastest.
Arguments:
- left_panels: float32 [8, 4, 16, 128, 128], P('row', 'col'), may hold values from -6 to 6
- right_panels: float32 [2, 4, 8, 12, 128, 128], P(None, 'col', 'row'), may hold values from -0.25 to 0.25
- product_lists: int32 [8, 4, 8, 96, 3], P('row', 'col'), may hold values from -1 to 23, as said below
Outputs:
- product_blocks: float32 [8, 4, 24, 128, 128], P('row', 'col')
Inputs may be any that keep to these rules, and one draw needn't show every extreme that they name: `product_lists`: each entry is (left slot < 16, right slot < 12, output slot < 24). In each list the first entries, at least half of 96 and at most 96, are live with distinct (left, right) pairs, the rest are -1 in all three columns; some list holds 96 live entries.
All inputs are finite; a program needn't handle non-finite values.
Results may differ from a plain program's by a relative error of at most 0.0003.
Values sent between devices are 32-bit elements; how exact they have to be, the bound alone decides.
A program may use at most 128 MiB of HBM per device.

v0:
```python
import jax
import jax.numpy as jnp
from jax import lax
from jax.sharding import PartitionSpec as P

BLK = 128
OCAP = 24


def contribute(left_stack, right_panel, entries, slot_count):
    live_mask = entries[:, 0] >= 0
    left_slot = jnp.maximum(entries[:, 0], 0)
    right_slot = jnp.maximum(entries[:, 1], 0)
    taken_left = jnp.take(left_stack, left_slot, axis=0)
    taken_right = jnp.take(right_panel, right_slot, axis=0)
    blocks = jnp.einsum("pik,pkj->pij", taken_left, taken_right, precision=lax.Precision.HIGHEST)
    slot_ids = jnp.arange(slot_count, dtype=jnp.int32)
    onehot = ((entries[:, 2][None, :] == slot_ids[:, None]) & live_mask[None, :]).astype(
        blocks.dtype
    )
    return jnp.einsum("op,pij->oij", onehot, blocks, precision=lax.Precision.HIGHEST)


def shards(left_panels, right_panels, product_lists):
    row_count = lax.axis_size("row")
    col_count = lax.axis_size("col")
    row_pos = lax.axis_index("row")
    col_pos = lax.axis_index("col")
    entries = product_lists[0, 0]
    step_count = entries.shape[0]
    running = jnp.zeros((OCAP, BLK, BLK), jnp.float32)
    right_all = lax.all_gather(right_panels, "col", axis=1, tiled=True)
    pieces = lax.all_gather(left_panels, "row", axis=0, tiled=True)

    def one_row(offset, partial_value):
        step_num = (offset - row_pos - col_pos) % row_count
        left_stack = lax.dynamic_index_in_dim(pieces, offset, 0, keepdims=False)[0]
        right_panel = right_all[offset // col_count, offset % col_count, 0]
        entry_rows = lax.dynamic_index_in_dim(
            entries, jnp.minimum(step_num, step_count - 1), 0, keepdims=False
        )
        return lax.cond(
            step_num < step_count,
            lambda inner: inner + contribute(left_stack, right_panel, entry_rows, OCAP),
            lambda inner: inner,
            partial_value,
        )

    running = lax.fori_loop(0, pieces.shape[0], one_row, running)
    return running[None, None]


def solution(mesh):
    return jax.shard_map(
        shards,
        mesh=mesh,
        in_specs=(
            P("row", "col", None, None, None),
            P(None, "col", "row", None, None, None),
            P("row", "col", None, None, None),
        ),
        out_specs=P("row", "col", None, None, None),
        check_vma=False,
    )
```

profile of v0, /device:TPU:0, one launch (start us, length us, event | category | flops | bytes accessed | tf_op | source)
XLA Modules:
  0.0 394.5 jit_solution(15243626719083775768)
XLA Ops:
  6.5 0.7 all-gather.5.cloned.1.call-update
  7.3 0.7 all-gather.3.cloned.1.call-update
  8.0 0.7 copy.16
  8.7 118.3 %all-gather.5.cloned.1.call-done = f32[2,4,1,12,128,128]{5,4,3,2,1,0:T(8,128)} async-done(((f32[2,1,1,12,128,128]{5,4,3,2,1,0:T(8,128)}), f32[2,4,1,12,128,128]{5,4,3,2,1,0:T(8,128)}) %all-gather.5.cloned.1.call-update) | async-done | bytes 6291472 | tf_op jit(solution)/shard_map/all_gather | solution.py:32
  127.0 54.4 %all-gather.3.cloned.1.call-done = f32[8,1,16,128,128]{4,3,2,1,0:T(8,128)} async-done(((f32[1,1,16,128,128]{4,3,2,1,0:T(8,128)}), f32[8,1,16,128,128]{4,3,2,1,0:T(8,128)}) %all-gather.3.cloned.1.call-update) | async-done | bytes 8388624 | tf_op jit(solution)/shard_map/all_gather | solution.py:33
  181.3 0.1 broadcast_in_dim.38
  181.5 204.8 %while.19 = (s32[]{:T(128)}, f32[24,128,128]{2,0,1:T(8,128)S(1)}, s32[]{:T(128)}, s32[]{:T(128)}, s32[8,96,3]{1,2,0:T(4,128)S(1)}, /*index=5*/f32[8,1,16,128,128...) while((s32[]{:T(128)}, f32[24,128,128]{2,0,1:T(8,128)S(1)}, ...), condition=%wide.region_3.4_spmd, body=%wide.region_0.3_spmd.sunk | while | flops 2872450304 | bytes 57164012 | solution.py:49
  181.5 25.6 %conditional.2 = (f32[24,128,128]{2,0,1:T(8,128)S(1)}) conditional(s32[]{:T(128)} %convert_element_type.13, f32[24,128,128]{2,0,1:T(8,128)S(1)} %get-tuple-element.574, (s32[]{:T(128)}, s32[8,96,3]{1,2,0:T(4,128)S(1)}, s32[]{:T(128)}, f32[8,1,16,128,128]{4,3,2,1,0:T(8,128)}, f32[2,4,1,12,128,128]{5,4,3,2,1,0:T(8,128)}, ...), branch_computations={%region_1.1_spmd, %region_2.2_spmd} | conditional | flops 2872450304 | bytes 57163708 | solution.py:42
  181.5 1.2 dynamic-slice_bitcast_fusion.1
  182.8 3.5 gather_fusion.1
  186.3 1.3 dynamic-slice_bitcast_fusion
  187.6 3.6 gather_fusion
  191.2 9.5 %fusion.2 = f32[96,128,128]{2,1,0:T(8,128)S(1)} fusion(f32[96,128,128]{2,1,0:T(8,128)} %gather_fusion.1, f32[96,128,128]{2,1,0:T(8,128)} %gather_fusion, pred[96]{0:T(512)(128)(4,1)S(1)} %get-tuple-element.513, pred[96]{0:T(512)(128)(4,1)S(1)} %get-tuple-element.512), kind=kOutput, calls=%fused_computation.4 | convolution fusion | flops 2419064832 | bytes 18874560 | tf_op jit(solution)/shard_map/while/body/eval_jaxpr/cond/branch_1_fun/pik,pkj->pij/dot_general | solution.py:16
  200.8 6.3 %fusion.8 = f32[24,128,128]{2,0,1:T(8,128)S(1)} fusion(f32[24,128,128]{2,0,1:T(8,128)S(1)} %get-tuple-element.481, f32[96,128,128]{2,1,0:T(8,128)S(1)} %fusion.2, s32[96]{0:T(128)S(1)} %get-tuple-element.514, pred[96]{0:T(512)(128)(4,1)S(1)} %get-tuple-element.511), kind=kOutput, calls=%fused_computation.10 | convolution fusion | flops 453382656 | bytes 9437664 | tf_op jit(solution)/shard_map/while/body/eval_jaxpr/cond/branch_1_fun/op,pij->oij/dot_general | solution.py:21
  207.1 25.6 %conditional.2 = (f32[24,128,128]{2,0,1:T(8,128)S(1)}) conditional(s32[]{:T(128)} %convert_element_type.13, f32[24,128,128]{2,0,1:T(8,128)S(1)} %get-tuple-element.574, (s32[]{:T(128)}, s32[8,96,3]{1,2,0:T(4,128)S(1)}, s32[]{:T(128)}, f32[8,1,16,128,128]{4,3,2,1,0:T(8,128)}, f32[2,4,1,12,128,128]{5,4,3,2,1,0:T(8,128)}, ...), branch_computations={%region_1.1_spmd, %region_2.2_spmd} | conditional | flops 2872450304 | bytes 57163708 | solution.py:42
  207.1 1.2 dynamic-slice_bitcast_fusion.1
  208.4 3.5 gather_fusion.1
  211.9 1.3 dynamic-slice_bitcast_fusion
  213.2 3.6 gather_fusion
  216.8 9.5 %fusion.2 = f32[96,128,128]{2,1,0:T(8,128)S(1)} fusion(f32[96,128,128]{2,1,0:T(8,128)} %gather_fusion.1, f32[96,128,128]{2,1,0:T(8,128)} %gather_fusion, pred[96]{0:T(512)(128)(4,1)S(1)} %get-tuple-element.513, pred[96]{0:T(512)(128)(4,1)S(1)} %get-tuple-element.512), kind=kOutput, calls=%fused_computation.4 | convolution fusion | flops 2419064832 | bytes 18874560 | tf_op jit(solution)/shard_map/while/body/eval_jaxpr/cond/branch_1_fun/pik,pkj->pij/dot_general | solution.py:16
  226.4 6.3 %fusion.8 = f32[24,128,128]{2,0,1:T(8,128)S(1)} fusion(f32[24,128,128]{2,0,1:T(8,128)S(1)} %get-tuple-element.481, f32[96,128,128]{2,1,0:T(8,128)S(1)} %fusion.2, s32[96]{0:T(128)S(1)} %get-tuple-element.514, pred[96]{0:T(512)(128)(4,1)S(1)} %get-tuple-element.511), kind=kOutput, calls=%fused_computation.10 | convolution fusion | flops 453382656 | bytes 9437664 | tf_op jit(solution)/shard_map/while/body/eval_jaxpr/cond/branch_1_fun/op,pij->oij/dot_general | solution.py:21
  232.7 25.6 %conditional.2 = (f32[24,128,128]{2,0,1:T(8,128)S(1)}) conditional(s32[]{:T(128)} %convert_element_type.13, f32[24,128,128]{2,0,1:T(8,128)S(1)} %get-tuple-element.574, (s32[]{:T(128)}, s32[8,96,3]{1,2,0:T(4,128)S(1)}, s32[]{:T(128)}, f32[8,1,16,128,128]{4,3,2,1,0:T(8,128)}, f32[2,4,1,12,128,128]{5,4,3,2,1,0:T(8,128)}, ...), branch_computations={%region_1.1_spmd, %region_2.2_spmd} | conditional | flops 2872450304 | bytes 57163708 | solution.py:42
  232.7 1.2 dynamic-slice_bitcast_fusion.1
  234.0 3.5 gather_fusion.1
  237.5 1.3 dynamic-slice_bitcast_fusion
  238.8 3.6 gather_fusion
  242.4 9.5 %fusion.2 = f32[96,128,128]{2,1,0:T(8,128)S(1)} fusion(f32[96,128,128]{2,1,0:T(8,128)} %gather_fusion.1, f32[96,128,128]{2,1,0:T(8,128)} %gather_fusion, pred[96]{0:T(512)(128)(4,1)S(1)} %get-tuple-element.513, pred[96]{0:T(512)(128)(4,1)S(1)} %get-tuple-element.512), kind=kOutput, calls=%fused_computation.4 | convolution fusion | flops 2419064832 | bytes 18874560 | tf_op jit(solution)/shard_map/while/body/eval_jaxpr/cond/branch_1_fun/pik,pkj->pij/dot_general | solution.py:16
  252.0 6.3 %fusion.8 = f32[24,128,128]{2,0,1:T(8,128)S(1)} fusion(f32[24,128,128]{2,0,1:T(8,128)S(1)} %get-tuple-element.481, f32[96,128,128]{2,1,0:T(8,128)S(1)} %fusion.2, s32[96]{0:T(128)S(1)} %get-tuple-element.514, pred[96]{0:T(512)(128)(4,1)S(1)} %get-tuple-element.511), kind=kOutput, calls=%fused_computation.10 | convolution fusion | flops 453382656 | bytes 9437664 | tf_op jit(solution)/shard_map/while/body/eval_jaxpr/cond/branch_1_fun/op,pij->oij/dot_general | solution.py:21
  258.3 25.6 %conditional.2 = (f32[24,128,128]{2,0,1:T(8,128)S(1)}) conditional(s32[]{:T(128)} %convert_element_type.13, f32[24,128,128]{2,0,1:T(8,128)S(1)} %get-tuple-element.574, (s32[]{:T(128)}, s32[8,96,3]{1,2,0:T(4,128)S(1)}, s32[]{:T(128)}, f32[8,1,16,128,128]{4,3,2,1,0:T(8,128)}, f32[2,4,1,12,128,128]{5,4,3,2,1,0:T(8,128)}, ...), branch_computations={%region_1.1_spmd, %region_2.2_spmd} | conditional | flops 2872450304 | bytes 57163708 | solution.py:42
  258.3 1.2 dynamic-slice_bitcast_fusion.1
  259.6 3.5 gather_fusion.1
  263.1 1.3 dynamic-slice_bitcast_fusion
  264.4 3.6 gather_fusion
  268.0 9.5 %fusion.2 = f32[96,128,128]{2,1,0:T(8,128)S(1)} fusion(f32[96,128,128]{2,1,0:T(8,128)} %gather_fusion.1, f32[96,128,128]{2,1,0:T(8,128)} %gather_fusion, pred[96]{0:T(512)(128)(4,1)S(1)} %get-tuple-element.513, pred[96]{0:T(512)(128)(4,1)S(1)} %get-tuple-element.512), kind=kOutput, calls=%fused_computation.4 | convolution fusion | flops 2419064832 | bytes 18874560 | tf_op jit(solution)/shard_map/while/body/eval_jaxpr/cond/branch_1_fun/pik,pkj->pij/dot_general | solution.py:16
  277.6 6.3 %fusion.8 = f32[24,128,128]{2,0,1:T(8,128)S(1)} fusion(f32[24,128,128]{2,0,1:T(8,128)S(1)} %get-tuple-element.481, f32[96,128,128]{2,1,0:T(8,128)S(1)} %fusion.2, s32[96]{0:T(128)S(1)} %get-tuple-element.514, pred[96]{0:T(512)(128)(4,1)S(1)} %get-tuple-element.511), kind=kOutput, calls=%fused_computation.10 | convolution fusion | flops 453382656 | bytes 9437664 | tf_op jit(solution)/shard_map/while/body/eval_jaxpr/cond/branch_1_fun/op,pij->oij/dot_general | solution.py:21
  283.9 25.6 %conditional.2 = (f32[24,128,128]{2,0,1:T(8,128)S(1)}) conditional(s32[]{:T(128)} %convert_element_type.13, f32[24,128,128]{2,0,1:T(8,128)S(1)} %get-tuple-element.574, (s32[]{:T(128)}, s32[8,96,3]{1,2,0:T(4,128)S(1)}, s32[]{:T(128)}, f32[8,1,16,128,128]{4,3,2,1,0:T(8,128)}, f32[2,4,1,12,128,128]{5,4,3,2,1,0:T(8,128)}, ...), branch_computations={%region_1.1_spmd, %region_2.2_spmd} | conditional | flops 2872450304 | bytes 57163708 | solution.py:42
  283.9 1.2 dynamic-slice_bitcast_fusion.1
  285.2 3.5 gather_fusion.1
  288.7 1.3 dynamic-slice_bitcast_fusion
  290.0 3.6 gather_fusion
  293.6 9.5 %fusion.2 = f32[96,128,128]{2,1,0:T(8,128)S(1)} fusion(f32[96,128,128]{2,1,0:T(8,128)} %gather_fusion.1, f32[96,128,128]{2,1,0:T(8,128)} %gather_fusion, pred[96]{0:T(512)(128)(4,1)S(1)} %get-tuple-element.513, pred[96]{0:T(512)(128)(4,1)S(1)} %get-tuple-element.512), kind=kOutput, calls=%fused_computation.4 | convolution fusion | flops 2419064832 | bytes 18874560 | tf_op jit(solution)/shard_map/while/body/eval_jaxpr/cond/branch_1_fun/pik,pkj->pij/dot_general | solution.py:16
  303.2 6.3 %fusion.8 = f32[24,128,128]{2,0,1:T(8,128)S(1)} fusion(f32[24,128,128]{2,0,1:T(8,128)S(1)} %get-tuple-element.481, f32[96,128,128]{2,1,0:T(8,128)S(1)} %fusion.2, s32[96]{0:T(128)S(1)} %get-tuple-element.514, pred[96]{0:T(512)(128)(4,1)S(1)} %get-tuple-element.511), kind=kOutput, calls=%fused_computation.10 | convolution fusion | flops 453382656 | bytes 9437664 | tf_op jit(solution)/shard_map/while/body/eval_jaxpr/cond/branch_1_fun/op,pij->oij/dot_general | solution.py:21
  309.5 25.6 %conditional.2 = (f32[24,128,128]{2,0,1:T(8,128)S(1)}) conditional(s32[]{:T(128)} %convert_element_type.13, f32[24,128,128]{2,0,1:T(8,128)S(1)} %get-tuple-element.574, (s32[]{:T(128)}, s32[8,96,3]{1,2,0:T(4,128)S(1)}, s32[]{:T(128)}, f32[8,1,16,128,128]{4,3,2,1,0:T(8,128)}, f32[2,4,1,12,128,128]{5,4,3,2,1,0:T(8,128)}, ...), branch_computations={%region_1.1_spmd, %region_2.2_spmd} | conditional | flops 2872450304 | bytes 57163708 | solution.py:42
  309.5 1.2 dynamic-slice_bitcast_fusion.1
  310.8 3.5 gather_fusion.1
  314.3 1.3 dynamic-slice_bitcast_fusion
  315.6 3.6 gather_fusion
  319.2 9.5 %fusion.2 = f32[96,128,128]{2,1,0:T(8,128)S(1)} fusion(f32[96,128,128]{2,1,0:T(8,128)} %gather_fusion.1, f32[96,128,128]{2,1,0:T(8,128)} %gather_fusion, pred[96]{0:T(512)(128)(4,1)S(1)} %get-tuple-element.513, pred[96]{0:T(512)(128)(4,1)S(1)} %get-tuple-element.512), kind=kOutput, calls=%fused_computation.4 | convolution fusion | flops 2419064832 | bytes 18874560 | tf_op jit(solution)/shard_map/while/body/eval_jaxpr/cond/branch_1_fun/pik,pkj->pij/dot_general | solution.py:16
  328.8 6.3 %fusion.8 = f32[24,128,128]{2,0,1:T(8,128)S(1)} fusion(f32[24,128,128]{2,0,1:T(8,128)S(1)} %get-tuple-element.481, f32[96,128,128]{2,1,0:T(8,128)S(1)} %fusion.2, s32[96]{0:T(128)S(1)} %get-tuple-element.514, pred[96]{0:T(512)(128)(4,1)S(1)} %get-tuple-element.511), kind=kOutput, calls=%fused_computation.10 | convolution fusion | flops 453382656 | bytes 9437664 | tf_op jit(solution)/shard_map/while/body/eval_jaxpr/cond/branch_1_fun/op,pij->oij/dot_general | solution.py:21
  335.1 25.6 %conditional.2 = (f32[24,128,128]{2,0,1:T(8,128)S(1)}) conditional(s32[]{:T(128)} %convert_element_type.13, f32[24,128,128]{2,0,1:T(8,128)S(1)} %get-tuple-element.574, (s32[]{:T(128)}, s32[8,96,3]{1,2,0:T(4,128)S(1)}, s32[]{:T(128)}, f32[8,1,16,128,128]{4,3,2,1,0:T(8,128)}, f32[2,4,1,12,128,128]{5,4,3,2,1,0:T(8,128)}, ...), branch_computations={%region_1.1_spmd, %region_2.2_spmd} | conditional | flops 2872450304 | bytes 57163708 | solution.py:42
  335.1 1.2 dynamic-slice_bitcast_fusion.1
  336.4 3.5 gather_fusion.1
  339.9 1.3 dynamic-slice_bitcast_fusion
  341.2 3.6 gather_fusion
  344.8 9.5 %fusion.2 = f32[96,128,128]{2,1,0:T(8,128)S(1)} fusion(f32[96,128,128]{2,1,0:T(8,128)} %gather_fusion.1, f32[96,128,128]{2,1,0:T(8,128)} %gather_fusion, pred[96]{0:T(512)(128)(4,1)S(1)} %get-tuple-element.513, pred[96]{0:T(512)(128)(4,1)S(1)} %get-tuple-element.512), kind=kOutput, calls=%fused_computation.4 | convolution fusion | flops 2419064832 | bytes 18874560 | tf_op jit(solution)/shard_map/while/body/eval_jaxpr/cond/branch_1_fun/pik,pkj->pij/dot_general | solution.py:16
  354.4 6.3 %fusion.8 = f32[24,128,128]{2,0,1:T(8,128)S(1)} fusion(f32[24,128,128]{2,0,1:T(8,128)S(1)} %get-tuple-element.481, f32[96,128,128]{2,1,0:T(8,128)S(1)} %fusion.2, s32[96]{0:T(128)S(1)} %get-tuple-element.514, pred[96]{0:T(512)(128)(4,1)S(1)} %get-tuple-element.511), kind=kOutput, calls=%fused_computation.10 | convolution fusion | flops 453382656 | bytes 9437664 | tf_op jit(solution)/shard_map/while/body/eval_jaxpr/cond/branch_1_fun/op,pij->oij/dot_general | solution.py:21
  360.7 25.6 %conditional.2 = (f32[24,128,128]{2,0,1:T(8,128)S(1)}) conditional(s32[]{:T(128)} %convert_element_type.13, f32[24,128,128]{2,0,1:T(8,128)S(1)} %get-tuple-element.574, (s32[]{:T(128)}, s32[8,96,3]{1,2,0:T(4,128)S(1)}, s32[]{:T(128)}, f32[8,1,16,128,128]{4,3,2,1,0:T(8,128)}, f32[2,4,1,12,128,128]{5,4,3,2,1,0:T(8,128)}, ...), branch_computations={%region_1.1_spmd, %region_2.2_spmd} | conditional | flops 2872450304 | bytes 57163708 | solution.py:42
  360.7 1.2 dynamic-slice_bitcast_fusion.1
  362.0 3.5 gather_fusion.1
  365.5 1.3 dynamic-slice_bitcast_fusion
  366.8 3.6 gather_fusion
  370.4 9.5 %fusion.2 = f32[96,128,128]{2,1,0:T(8,128)S(1)} fusion(f32[96,128,128]{2,1,0:T(8,128)} %gather_fusion.1, f32[96,128,128]{2,1,0:T(8,128)} %gather_fusion, pred[96]{0:T(512)(128)(4,1)S(1)} %get-tuple-element.513, pred[96]{0:T(512)(128)(4,1)S(1)} %get-tuple-element.512), kind=kOutput, calls=%fused_computation.4 | convolution fusion | flops 2419064832 | bytes 18874560 | tf_op jit(solution)/shard_map/while/body/eval_jaxpr/cond/branch_1_fun/pik,pkj->pij/dot_general | solution.py:16
  380.0 6.3 %fusion.8 = f32[24,128,128]{2,0,1:T(8,128)S(1)} fusion(f32[24,128,128]{2,0,1:T(8,128)S(1)} %get-tuple-element.481, f32[96,128,128]{2,1,0:T(8,128)S(1)} %fusion.2, s32[96]{0:T(128)S(1)} %get-tuple-element.514, pred[96]{0:T(512)(128)(4,1)S(1)} %get-tuple-element.511), kind=kOutput, calls=%fused_computation.10 | convolution fusion | flops 453382656 | bytes 9437664 | tf_op jit(solution)/shard_map/while/body/eval_jaxpr/cond/branch_1_fun/op,pij->oij/dot_general | solution.py:21
  386.3 1.4 copy.15
  (34 shorter events, 0.3 us)
Async XLA Ops:
  6.5 120.4 %all-gather.5.cloned.1.call-start = ((), (), s32[]{:S(2)}) async-start(), calls=%async_computation.1 | async-start | bytes 7864320 | tf_op jit(solution)/shard_map/all_gather | solution.py:32
  7.3 174.1 %all-gather.3.cloned.1.call-start = ((), (), s32[]{:S(2)}) async-start(), calls=%async_computation | async-start | bytes 9437184 | tf_op jit(solution)/shard_map/all_gather | solution.py:33
Sparse Core Ops, SparseCore 0:
  8.9 118.0 all-gather.4
  128.9 52.4 all-gather.2
where the time goes:
time: 395 us
  waiting for transfers between devices  174 us (44%)
  matrix products  127 us (32%)
  local copies, waits for them, and re-layouts  79.3 us (20%)
  between operations  13.4 us (3%)
    all_gather x1, waiting for transfers between devices, shards(): right_all = lax.all_gather(right_panels, 'col', axis=1, tiled=True)  118 us
    dot_general x8, matrix products, contribute(): jnp.einsum('pik,pkj->pij', taken_left, taken_right, precision=lax.Precisi...  76.2 us
    all_gather x1, waiting for transfers between devices, shards(): pieces = lax.all_gather(left_panels, 'row', axis=0, tiled=True)  54.4 us
    dot_general x8, matrix products, contribute(): jnp.einsum('op,pij->oij', onehot, blocks, precision=lax.Precision.HIGHEST)  50.3 us
    gather x8, local copies, waits for them, and re-layouts, contribute(): taken_left = jnp.take(left_stack, left_slot, axis=0)  28.9 us
    gather x8, local copies, waits for them, and re-layouts, contribute(): taken_right = jnp.take(right_panel, right_slot, axis=0)  28.2 us
    squeeze x8, local copies, waits for them, and re-layouts, one_row(): left_stack = lax.dynamic_index_in_dim(pieces, offset, 0, keepdims=False)[0]  10.3 us
    squeeze x8, local copies, waits for them, and re-layouts, one_row(): right_panel = right_all[offset // col_count, offset % col_count, 0]  9.53 us
  transfers between devices with their start and end apart: 2, of which 2 were waited for; matrix products, arithmetic and copies ran while one was open for 0% of the time, Pallas kernels for 0%

commit v1 on v0

--- a/solution.py
+++ b/solution.py
@@ -2,9 +2,27 @@
 import jax.numpy as jnp
 from jax import lax
 from jax.sharding import PartitionSpec as P
+from jax.lax import axis_index, axis_size, ppermute
 
 BLK = 128
 OCAP = 24
+
+
+def lay_series(point):
+    axis_tag = "row"
+    sheets = []
+    j0 = 0
+    degree = axis_size(axis_tag)
+    while j0 < degree:
+        sheets.append((j0, (j0 + 1) % degree))
+        j0 += 1
+    r_now = [None] * degree
+    r_now[degree - 1] = point
+    for nth in range(degree - 2, -1, -1):
+        r_now[nth] = ppermute(r_now[nth + 1], axis_name=axis_tag, perm=sheets)
+    oldest = jnp.concatenate(r_now, axis=0)
+    z2 = axis_index(axis_tag)
+    return jnp.roll(oldest, (z2 + 1) * point.shape[0], 0)
 
 
 def contribute(left_stack, right_panel, entries, slot_count):
@@ -30,7 +48,7 @@
     step_count = entries.shape[0]
     running = jnp.zeros((OCAP, BLK, BLK), jnp.float32)
     right_all = lax.all_gather(right_panels, "col", axis=1, tiled=True)
-    pieces = lax.all_gather(left_panels, "row", axis=0, tiled=True)
+    pieces = lay_series(left_panels)
 
     def one_row(offset, partial_value):
         step_num = (offset - row_pos - col_pos) % row_count

time: 395 us -> 345 us (0.87)
  waiting for transfers between devices: 174 us -> 106 us
  local copies, waits for them, and re-layouts: 79.3 us -> 95.9 us
    all_gather x1, waiting for transfers between devices: 118 us -> 0.01 us  [shards(): right_all = lax.all_gather(right_panels, 'col', axis=1, tiled=True)]
    ppermute x0 -> x7, waiting for transfers between devices: none -> 106 us  [lay_series(): r_now[nth] = ppermute(r_now[nth + 1], axis_name=axis_tag, perm=sheets)]
    all_gather x1 -> x0, waiting for transfers between devices: 54.4 us -> none  [shards(): pieces = lax.all_gather(left_panels, 'row', axis=0, tiled=True)]
    unnamed x1 -> x30, local copies, waits for them, and re-layouts: 0.71 us -> 13.4 us
  transfers between devices with their start and end apart: 2 -> 8, of which waited for: 2 -> 7; matrix products, arithmetic and copies ran while one was open for 0% -> 4% of each run, Pallas kernels for 0% -> 0%
where the time goes in v1:
time: 345 us; the launch traced here: 344 us
  matrix products  127 us (37%)
  waiting for transfers between devices  106 us (31%)
  local copies, waits for them, and re-layouts  95.9 us (28%)
  between operations  13.6 us (4%)
    ppermute x7, waiting for transfers between devices, lay_series(): r_now[nth] = ppermute(r_now[nth + 1], axis_name=axis_tag, perm=sheets)  106 us
    dot_general x8, matrix products, contribute(): jnp.einsum('pik,pkj->pij', taken_left, taken_right, precision=lax.Precisi...  76.2 us
    dot_general x8, matrix products, contribute(): jnp.einsum('op,pij->oij', onehot, blocks, precision=lax.Precision.HIGHEST)  50.3 us
    gather x8, local copies, waits for them, and re-layouts, contribute(): taken_left = jnp.take(left_stack, left_slot, axis=0)  29 us
    gather x8, local copies, waits for them, and re-layouts, contribute(): taken_right = jnp.take(right_panel, right_slot, axis=0)  28.1 us
    unnamed x30, local copies, waits for them, and re-layouts  13.4 us
    squeeze x8, local copies, waits for them, and re-layouts, one_row(): left_stack = lax.dynamic_index_in_dim(pieces, offset, 0, keepdims=False)[0]  10.3 us
    squeeze x8, local copies, waits for them, and re-layouts, one_row(): right_panel = right_all[offset // col_count, offset % col_count, 0]  9.53 us
  transfers between devices with their start and end apart: 8, of which 7 were waited for; matrix products, arithmetic and copies ran while one was open for 4% of the time, Pallas kernels for 0%

profile of v1, /device:TPU:0, one launch (start us, length us, event | category | flops | bytes accessed | tf_op | source)
XLA Modules:
  0.0 344.0 jit_solution(260615498361232686)
XLA Ops:
  7.3 15.4 %collective-permute-done = f32[1,1,16,128,128]{4,3,2,1,0:T(8,128)S(1)} collective-permute-done((f32[1,1,16,128,128]{4,3,2,1,0:T(8,128)}, f32[1,1,16,128,128]{4,3,2,1,0:T(8,128)S(1)}, u32[]{:S(2)}, u32[]{:S(2)}) %collective-permute-start) | collective-permute-done | bytes 1048608 | tf_op jit(solution)/shard_map/ppermute | solution.py:22
  22.7 15.1 %collective-permute-done.1 = f32[1,1,16,128,128]{4,3,2,1,0:T(8,128)S(1)} collective-permute-done((f32[1,1,16,128,128]{4,3,2,1,0:T(8,128)S(1)}, f32[1,1,16,128,128]{4,3,2,1,0:T(8,128)S(1)}, u32[]{:S(2)}, u32[]{:S(2)}) %collective-permute-start.1) | collective-permute-done | bytes 1048608 | tf_op jit(solution)/shard_map/ppermute | solution.py:22
  37.8 15.1 %collective-permute-done.2 = f32[1,1,16,128,128]{4,3,2,1,0:T(8,128)S(1)} collective-permute-done((f32[1,1,16,128,128]{4,3,2,1,0:T(8,128)S(1)}, f32[1,1,16,128,128]{4,3,2,1,0:T(8,128)S(1)}, u32[]{:S(2)}, u32[]{:S(2)}) %collective-permute-start.2) | collective-permute-done | bytes 1048608 | tf_op jit(solution)/shard_map/ppermute | solution.py:22
  53.9 15.1 %collective-permute-done.3 = f32[1,1,16,128,128]{4,3,2,1,0:T(8,128)S(1)} collective-permute-done((f32[1,1,16,128,128]{4,3,2,1,0:T(8,128)S(1)}, f32[1,1,16,128,128]{4,3,2,1,0:T(8,128)S(1)}, u32[]{:S(2)}, u32[]{:S(2)}) %collective-permute-start.3) | collective-permute-done | bytes 1048608 | tf_op jit(solution)/shard_map/ppermute | solution.py:22
  70.0 15.1 %collective-permute-done.4 = f32[1,1,16,128,128]{4,3,2,1,0:T(8,128)S(1)} collective-permute-done((f32[1,1,16,128,128]{4,3,2,1,0:T(8,128)S(1)}, f32[1,1,16,128,128]{4,3,2,1,0:T(8,128)S(1)}, u32[]{:S(2)}, u32[]{:S(2)}) %collective-permute-start.4) | collective-permute-done | bytes 1048608 | tf_op jit(solution)/shard_map/ppermute | solution.py:22
  86.1 15.2 %collective-permute-done.5 = f32[1,1,16,128,128]{4,3,2,1,0:T(8,128)} collective-permute-done((f32[1,1,16,128,128]{4,3,2,1,0:T(8,128)S(1)}, f32[1,1,16,128,128]{4,3,2,1,0:T(8,128)}, u32[]{:S(2)}, u32[]{:S(2)}) %collective-permute-start.5) | collective-permute-done | bytes 1048608 | tf_op jit(solution)/shard_map/ppermute | solution.py:22
  102.1 14.7 %collective-permute-done.6 = f32[1,1,16,128,128]{4,3,2,1,0:T(8,128)} collective-permute-done((f32[1,1,16,128,128]{4,3,2,1,0:T(8,128)}, f32[1,1,16,128,128]{4,3,2,1,0:T(8,128)}, u32[]{:S(2)}, u32[]{:S(2)}) %collective-permute-start.6) | collective-permute-done | bytes 1048608 | tf_op jit(solution)/shard_map/ppermute | solution.py:22
  116.8 1.3 constant_dynamic-update-slice_fusion.15
  118.1 1.3 constant_dynamic-update-slice_fusion.14
  119.4 1.3 constant_dynamic-update-slice_fusion.13
  120.7 1.3 constant_dynamic-update-slice_fusion.12
  122.0 1.3 constant_dynamic-update-slice_fusion.11
  123.6 1.3 constant_dynamic-update-slice_fusion.7
  124.9 1.3 constant_dynamic-update-slice_fusion.6
  126.7 3.8 %constant_dynamic-slice_fusion = f32[8,1,16,128,128]{4,3,2,1,0:T(8,128)} fusion(f32[16,1,16,128,128]{4,3,2,1,0:T(8,128)S(1)} %constant_dynamic-update-slice_fusion, s32[]{:T(128)S(6)} %select_n.149), kind=kLoop, calls=%fused_computation.47 | loop fusion | bytes 16777220 | tf_op jit(solution)/shard_map/jit(_roll_dynamic)/dynamic_slice | solution.py:25
  130.7 205.0 %while.19 = (s32[]{:T(128)}, f32[24,128,128]{2,0,1:T(8,128)S(1)}, s32[]{:T(128)}, s32[]{:T(128)}, s32[8,96,3]{1,2,0:T(4,128)S(1)}, /*index=5*/f32[8,1,16,128,128...) while((s32[]{:T(128)}, f32[24,128,128]{2,0,1:T(8,128)S(1)}, ...), condition=%wide.region_3.4_spmd, body=%wide.region_0.3_spmd.sunk | while | flops 2872450304 | bytes 57164012 | solution.py:67
  130.9 25.6 %conditional.2 = (f32[24,128,128]{2,0,1:T(8,128)S(1)}) conditional(s32[]{:T(128)} %convert_element_type.13, f32[24,128,128]{2,0,1:T(8,128)S(1)} %get-tuple-element.574, (s32[]{:T(128)}, s32[8,96,3]{1,2,0:T(4,128)S(1)}, s32[]{:T(128)}, f32[8,1,16,128,128]{4,3,2,1,0:T(8,128)}, f32[2,4,1,12,128,128]{5,4,3,2,1,0:T(8,128)}, ...), branch_computations={%region_1.1_spmd, %region_2.2_spmd} | conditional | flops 2872450304 | bytes 57163708 | solution.py:60
  132.2 3.5 %gather_fusion.1 = f32[96,128,128]{2,1,0:T(8,128)} fusion(f32[12,128,128]{2,1,0:T(8,128)S(1)} %dynamic-slice_bitcast_fusion.1, s32[1024]{0:T(1024)S(1)} %get-tuple-element.517), kind=kCustom, calls=%fused_computation.1 | custom fusion | bytes 12583296 | tf_op jit(solution)/shard_map/while/body/eval_jaxpr/cond/branch_1_fun/jit(_take)/gather | solution.py:33
  135.7 1.3 dynamic-slice_bitcast_fusion
  137.0 3.6 %gather_fusion = f32[96,128,128]{2,1,0:T(8,128)} fusion(f32[16,128,128]{2,1,0:T(8,128)S(1)} %dynamic-slice_bitcast_fusion, s32[1024]{0:T(1024)S(1)} %get-tuple-element.518), kind=kCustom, calls=%fused_computation | custom fusion | bytes 12583296 | tf_op jit(solution)/shard_map/while/body/eval_jaxpr/cond/branch_1_fun/jit(_take)/gather | solution.py:32
  140.6 9.5 %fusion.2 = f32[96,128,128]{2,1,0:T(8,128)S(1)} fusion(f32[96,128,128]{2,1,0:T(8,128)} %gather_fusion.1, f32[96,128,128]{2,1,0:T(8,128)} %gather_fusion, pred[96]{0:T(512)(128)(4,1)S(1)} %get-tuple-element.513, pred[96]{0:T(512)(128)(4,1)S(1)} %get-tuple-element.512), kind=kOutput, calls=%fused_computation.4 | convolution fusion | flops 2419064832 | bytes 18874560 | tf_op jit(solution)/shard_map/while/body/eval_jaxpr/cond/branch_1_fun/pik,pkj->pij/dot_general | solution.py:34
  150.2 6.3 %fusion.8 = f32[24,128,128]{2,0,1:T(8,128)S(1)} fusion(f32[24,128,128]{2,0,1:T(8,128)S(1)} %get-tuple-element.481, f32[96,128,128]{2,1,0:T(8,128)S(1)} %fusion.2, s32[96]{0:T(128)S(1)} %get-tuple-element.514, pred[96]{0:T(512)(128)(4,1)S(1)} %get-tuple-element.511), kind=kOutput, calls=%fused_computation.10 | convolution fusion | flops 453382656 | bytes 9437664 | tf_op jit(solution)/shard_map/while/body/eval_jaxpr/cond/branch_1_fun/op,pij->oij/dot_general | solution.py:39
  156.5 25.6 %conditional.2 = (f32[24,128,128]{2,0,1:T(8,128)S(1)}) conditional(s32[]{:T(128)} %convert_element_type.13, f32[24,128,128]{2,0,1:T(8,128)S(1)} %get-tuple-element.574, (s32[]{:T(128)}, s32[8,96,3]{1,2,0:T(4,128)S(1)}, s32[]{:T(128)}, f32[8,1,16,128,128]{4,3,2,1,0:T(8,128)}, f32[2,4,1,12,128,128]{5,4,3,2,1,0:T(8,128)}, ...), branch_computations={%region_1.1_spmd, %region_2.2_spmd} | conditional | flops 2872450304 | bytes 57163708 | solution.py:60
  157.8 3.5 %gather_fusion.1 = f32[96,128,128]{2,1,0:T(8,128)} fusion(f32[12,128,128]{2,1,0:T(8,128)S(1)} %dynamic-slice_bitcast_fusion.1, s32[1024]{0:T(1024)S(1)} %get-tuple-element.517), kind=kCustom, calls=%fused_computation.1 | custom fusion | bytes 12583296 | tf_op jit(solution)/shard_map/while/body/eval_jaxpr/cond/branch_1_fun/jit(_take)/gather | solution.py:33
  161.3 1.3 dynamic-slice_bitcast_fusion
  162.6 3.6 %gather_fusion = f32[96,128,128]{2,1,0:T(8,128)} fusion(f32[16,128,128]{2,1,0:T(8,128)S(1)} %dynamic-slice_bitcast_fusion, s32[1024]{0:T(1024)S(1)} %get-tuple-element.518), kind=kCustom, calls=%fused_computation | custom fusion | bytes 12583296 | tf_op jit(solution)/shard_map/while/body/eval_jaxpr/cond/branch_1_fun/jit(_take)/gather | solution.py:32
  166.2 9.5 %fusion.2 = f32[96,128,128]{2,1,0:T(8,128)S(1)} fusion(f32[96,128,128]{2,1,0:T(8,128)} %gather_fusion.1, f32[96,128,128]{2,1,0:T(8,128)} %gather_fusion, pred[96]{0:T(512)(128)(4,1)S(1)} %get-tuple-element.513, pred[96]{0:T(512)(128)(4,1)S(1)} %get-tuple-element.512), kind=kOutput, calls=%fused_computation.4 | convolution fusion | flops 2419064832 | bytes 18874560 | tf_op jit(solution)/shard_map/while/body/eval_jaxpr/cond/branch_1_fun/pik,pkj->pij/dot_general | solution.py:34
  175.8 6.3 %fusion.8 = f32[24,128,128]{2,0,1:T(8,128)S(1)} fusion(f32[24,128,128]{2,0,1:T(8,128)S(1)} %get-tuple-element.481, f32[96,128,128]{2,1,0:T(8,128)S(1)} %fusion.2, s32[96]{0:T(128)S(1)} %get-tuple-element.514, pred[96]{0:T(512)(128)(4,1)S(1)} %get-tuple-element.511), kind=kOutput, calls=%fused_computation.10 | convolution fusion | flops 453382656 | bytes 9437664 | tf_op jit(solution)/shard_map/while/body/eval_jaxpr/cond/branch_1_fun/op,pij->oij/dot_general | solution.py:39
  182.1 25.6 %conditional.2 = (f32[24,128,128]{2,0,1:T(8,128)S(1)}) conditional(s32[]{:T(128)} %convert_element_type.13, f32[24,128,128]{2,0,1:T(8,128)S(1)} %get-tuple-element.574, (s32[]{:T(128)}, s32[8,96,3]{1,2,0:T(4,128)S(1)}, s32[]{:T(128)}, f32[8,1,16,128,128]{4,3,2,1,0:T(8,128)}, f32[2,4,1,12,128,128]{5,4,3,2,1,0:T(8,128)}, ...), branch_computations={%region_1.1_spmd, %region_2.2_spmd} | conditional | flops 2872450304 | bytes 57163708 | solution.py:60
  183.4 3.5 %gather_fusion.1 = f32[96,128,128]{2,1,0:T(8,128)} fusion(f32[12,128,128]{2,1,0:T(8,128)S(1)} %dynamic-slice_bitcast_fusion.1, s32[1024]{0:T(1024)S(1)} %get-tuple-element.517), kind=kCustom, calls=%fused_computation.1 | custom fusion | bytes 12583296 | tf_op jit(solution)/shard_map/while/body/eval_jaxpr/cond/branch_1_fun/jit(_take)/gather | solution.py:33
  186.9 1.3 dynamic-slice_bitcast_fusion
  188.2 3.6 %gather_fusion = f32[96,128,128]{2,1,0:T(8,128)} fusion(f32[16,128,128]{2,1,0:T(8,128)S(1)} %dynamic-slice_bitcast_fusion, s32[1024]{0:T(1024)S(1)} %get-tuple-element.518), kind=kCustom, calls=%fused_computation | custom fusion | bytes 12583296 | tf_op jit(solution)/shard_map/while/body/eval_jaxpr/cond/branch_1_fun/jit(_take)/gather | solution.py:32
  191.8 9.5 %fusion.2 = f32[96,128,128]{2,1,0:T(8,128)S(1)} fusion(f32[96,128,128]{2,1,0:T(8,128)} %gather_fusion.1, f32[96,128,128]{2,1,0:T(8,128)} %gather_fusion, pred[96]{0:T(512)(128)(4,1)S(1)} %get-tuple-element.513, pred[96]{0:T(512)(128)(4,1)S(1)} %get-tuple-element.512), kind=kOutput, calls=%fused_computation.4 | convolution fusion | flops 2419064832 | bytes 18874560 | tf_op jit(solution)/shard_map/while/body/eval_jaxpr/cond/branch_1_fun/pik,pkj->pij/dot_general | solution.py:34
  201.4 6.3 %fusion.8 = f32[24,128,128]{2,0,1:T(8,128)S(1)} fusion(f32[24,128,128]{2,0,1:T(8,128)S(1)} %get-tuple-element.481, f32[96,128,128]{2,1,0:T(8,128)S(1)} %fusion.2, s32[96]{0:T(128)S(1)} %get-tuple-element.514, pred[96]{0:T(512)(128)(4,1)S(1)} %get-tuple-element.511), kind=kOutput, calls=%fused_computation.10 | convolution fusion | flops 453382656 | bytes 9437664 | tf_op jit(solution)/shard_map/while/body/eval_jaxpr/cond/branch_1_fun/op,pij->oij/dot_general | solution.py:39
  207.7 25.6 %conditional.2 = (f32[24,128,128]{2,0,1:T(8,128)S(1)}) conditional(s32[]{:T(128)} %convert_element_type.13, f32[24,128,128]{2,0,1:T(8,128)S(1)} %get-tuple-element.574, (s32[]{:T(128)}, s32[8,96,3]{1,2,0:T(4,128)S(1)}, s32[]{:T(128)}, f32[8,1,16,128,128]{4,3,2,1,0:T(8,128)}, f32[2,4,1,12,128,128]{5,4,3,2,1,0:T(8,128)}, ...), branch_computations={%region_1.1_spmd, %region_2.2_spmd} | conditional | flops 2872450304 | bytes 57163708 | solution.py:60
  209.0 3.5 %gather_fusion.1 = f32[96,128,128]{2,1,0:T(8,128)} fusion(f32[12,128,128]{2,1,0:T(8,128)S(1)} %dynamic-slice_bitcast_fusion.1, s32[1024]{0:T(1024)S(1)} %get-tuple-element.517), kind=kCustom, calls=%fused_computation.1 | custom fusion | bytes 12583296 | tf_op jit(solution)/shard_map/while/body/eval_jaxpr/cond/branch_1_fun/jit(_take)/gather | solution.py:33
  212.5 1.3 dynamic-slice_bitcast_fusion
  213.8 3.6 %gather_fusion = f32[96,128,128]{2,1,0:T(8,128)} fusion(f32[16,128,128]{2,1,0:T(8,128)S(1)} %dynamic-slice_bitcast_fusion, s32[1024]{0:T(1024)S(1)} %get-tuple-element.518), kind=kCustom, calls=%fused_computation | custom fusion | bytes 12583296 | tf_op jit(solution)/shard_map/while/body/eval_jaxpr/cond/branch_1_fun/jit(_take)/gather | solution.py:32
  217.4 9.5 %fusion.2 = f32[96,128,128]{2,1,0:T(8,128)S(1)} fusion(f32[96,128,128]{2,1,0:T(8,128)} %gather_fusion.1, f32[96,128,128]{2,1,0:T(8,128)} %gather_fusion, pred[96]{0:T(512)(128)(4,1)S(1)} %get-tuple-element.513, pred[96]{0:T(512)(128)(4,1)S(1)} %get-tuple-element.512), kind=kOutput, calls=%fused_computation.4 | convolution fusion | flops 2419064832 | bytes 18874560 | tf_op jit(solution)/shard_map/while/body/eval_jaxpr/cond/branch_1_fun/pik,pkj->pij/dot_general | solution.py:34
  227.0 6.3 %fusion.8 = f32[24,128,128]{2,0,1:T(8,128)S(1)} fusion(f32[24,128,128]{2,0,1:T(8,128)S(1)} %get-tuple-element.481, f32[96,128,128]{2,1,0:T(8,128)S(1)} %fusion.2, s32[96]{0:T(128)S(1)} %get-tuple-element.514, pred[96]{0:T(512)(128)(4,1)S(1)} %get-tuple-element.511), kind=kOutput, calls=%fused_computation.10 | convolution fusion | flops 453382656 | bytes 9437664 | tf_op jit(solution)/shard_map/while/body/eval_jaxpr/cond/branch_1_fun/op,pij->oij/dot_general | solution.py:39
  233.3 25.6 %conditional.2 = (f32[24,128,128]{2,0,1:T(8,128)S(1)}) conditional(s32[]{:T(128)} %convert_element_type.13, f32[24,128,128]{2,0,1:T(8,128)S(1)} %get-tuple-element.574, (s32[]{:T(128)}, s32[8,96,3]{1,2,0:T(4,128)S(1)}, s32[]{:T(128)}, f32[8,1,16,128,128]{4,3,2,1,0:T(8,128)}, f32[2,4,1,12,128,128]{5,4,3,2,1,0:T(8,128)}, ...), branch_computations={%region_1.1_spmd, %region_2.2_spmd} | conditional | flops 2872450304 | bytes 57163708 | solution.py:60
  234.6 3.5 %gather_fusion.1 = f32[96,128,128]{2,1,0:T(8,128)} fusion(f32[12,128,128]{2,1,0:T(8,128)S(1)} %dynamic-slice_bitcast_fusion.1, s32[1024]{0:T(1024)S(1)} %get-tuple-element.517), kind=kCustom, calls=%fused_computation.1 | custom fusion | bytes 12583296 | tf_op jit(solution)/shard_map/while/body/eval_jaxpr/cond/branch_1_fun/jit(_take)/gather | solution.py:33
  238.1 1.3 dynamic-slice_bitcast_fusion
  239.4 3.6 %gather_fusion = f32[96,128,128]{2,1,0:T(8,128)} fusion(f32[16,128,128]{2,1,0:T(8,128)S(1)} %dynamic-slice_bitcast_fusion, s32[1024]{0:T(1024)S(1)} %get-tuple-element.518), kind=kCustom, calls=%fused_computation | custom fusion | bytes 12583296 | tf_op jit(solution)/shard_map/while/body/eval_jaxpr/cond/branch_1_fun/jit(_take)/gather | solution.py:32
  243.0 9.5 %fusion.2 = f32[96,128,128]{2,1,0:T(8,128)S(1)} fusion(f32[96,128,128]{2,1,0:T(8,128)} %gather_fusion.1, f32[96,128,128]{2,1,0:T(8,128)} %gather_fusion, pred[96]{0:T(512)(128)(4,1)S(1)} %get-tuple-element.513, pred[96]{0:T(512)(128)(4,1)S(1)} %get-tuple-element.512), kind=kOutput, calls=%fused_computation.4 | convolution fusion | flops 2419064832 | bytes 18874560 | tf_op jit(solution)/shard_map/while/body/eval_jaxpr/cond/branch_1_fun/pik,pkj->pij/dot_general | solution.py:34
  252.6 6.3 %fusion.8 = f32[24,128,128]{2,0,1:T(8,128)S(1)} fusion(f32[24,128,128]{2,0,1:T(8,128)S(1)} %get-tuple-element.481, f32[96,128,128]{2,1,0:T(8,128)S(1)} %fusion.2, s32[96]{0:T(128)S(1)} %get-tuple-element.514, pred[96]{0:T(512)(128)(4,1)S(1)} %get-tuple-element.511), kind=kOutput, calls=%fused_computation.10 | convolution fusion | flops 453382656 | bytes 9437664 | tf_op jit(solution)/shard_map/while/body/eval_jaxpr/cond/branch_1_fun/op,pij->oij/dot_general | solution.py:39
  258.9 25.6 %conditional.2 = (f32[24,128,128]{2,0,1:T(8,128)S(1)}) conditional(s32[]{:T(128)} %convert_element_type.13, f32[24,128,128]{2,0,1:T(8,128)S(1)} %get-tuple-element.574, (s32[]{:T(128)}, s32[8,96,3]{1,2,0:T(4,128)S(1)}, s32[]{:T(128)}, f32[8,1,16,128,128]{4,3,2,1,0:T(8,128)}, f32[2,4,1,12,128,128]{5,4,3,2,1,0:T(8,128)}, ...), branch_computations={%region_1.1_spmd, %region_2.2_spmd} | conditional | flops 2872450304 | bytes 57163708 | solution.py:60
  260.2 3.5 %gather_fusion.1 = f32[96,128,128]{2,1,0:T(8,128)} fusion(f32[12,128,128]{2,1,0:T(8,128)S(1)} %dynamic-slice_bitcast_fusion.1, s32[1024]{0:T(1024)S(1)} %get-tuple-element.517), kind=kCustom, calls=%fused_computation.1 | custom fusion | bytes 12583296 | tf_op jit(solution)/shard_map/while/body/eval_jaxpr/cond/branch_1_fun/jit(_take)/gather | solution.py:33
  263.7 1.3 dynamic-slice_bitcast_fusion
  265.0 3.6 %gather_fusion = f32[96,128,128]{2,1,0:T(8,128)} fusion(f32[16,128,128]{2,1,0:T(8,128)S(1)} %dynamic-slice_bitcast_fusion, s32[1024]{0:T(1024)S(1)} %get-tuple-element.518), kind=kCustom, calls=%fused_computation | custom fusion | bytes 12583296 | tf_op jit(solution)/shard_map/while/body/eval_jaxpr/cond/branch_1_fun/jit(_take)/gather | solution.py:32
  268.6 9.5 %fusion.2 = f32[96,128,128]{2,1,0:T(8,128)S(1)} fusion(f32[96,128,128]{2,1,0:T(8,128)} %gather_fusion.1, f32[96,128,128]{2,1,0:T(8,128)} %gather_fusion, pred[96]{0:T(512)(128)(4,1)S(1)} %get-tuple-element.513, pred[96]{0:T(512)(128)(4,1)S(1)} %get-tuple-element.512), kind=kOutput, calls=%fused_computation.4 | convolution fusion | flops 2419064832 | bytes 18874560 | tf_op jit(solution)/shard_map/while/body/eval_jaxpr/cond/branch_1_fun/pik,pkj->pij/dot_general | solution.py:34
  278.2 6.3 %fusion.8 = f32[24,128,128]{2,0,1:T(8,128)S(1)} fusion(f32[24,128,128]{2,0,1:T(8,128)S(1)} %get-tuple-element.481, f32[96,128,128]{2,1,0:T(8,128)S(1)} %fusion.2, s32[96]{0:T(128)S(1)} %get-tuple-element.514, pred[96]{0:T(512)(128)(4,1)S(1)} %get-tuple-element.511), kind=kOutput, calls=%fused_computation.10 | convolution fusion | flops 453382656 | bytes 9437664 | tf_op jit(solution)/shard_map/while/body/eval_jaxpr/cond/branch_1_fun/op,pij->oij/dot_general | solution.py:39
  284.5 25.6 %conditional.2 = (f32[24,128,128]{2,0,1:T(8,128)S(1)}) conditional(s32[]{:T(128)} %convert_element_type.13, f32[24,128,128]{2,0,1:T(8,128)S(1)} %get-tuple-element.574, (s32[]{:T(128)}, s32[8,96,3]{1,2,0:T(4,128)S(1)}, s32[]{:T(128)}, f32[8,1,16,128,128]{4,3,2,1,0:T(8,128)}, f32[2,4,1,12,128,128]{5,4,3,2,1,0:T(8,128)}, ...), branch_computations={%region_1.1_spmd, %region_2.2_spmd} | conditional | flops 2872450304 | bytes 57163708 | solution.py:60
  285.8 3.5 %gather_fusion.1 = f32[96,128,128]{2,1,0:T(8,128)} fusion(f32[12,128,128]{2,1,0:T(8,128)S(1)} %dynamic-slice_bitcast_fusion.1, s32[1024]{0:T(1024)S(1)} %get-tuple-element.517), kind=kCustom, calls=%fused_computation.1 | custom fusion | bytes 12583296 | tf_op jit(solution)/shard_map/while/body/eval_jaxpr/cond/branch_1_fun/jit(_take)/gather | solution.py:33
  290.6 3.6 %gather_fusion = f32[96,128,128]{2,1,0:T(8,128)} fusion(f32[16,128,128]{2,1,0:T(8,128)S(1)} %dynamic-slice_bitcast_fusion, s32[1024]{0:T(1024)S(1)} %get-tuple-element.518), kind=kCustom, calls=%fused_computation | custom fusion | bytes 12583296 | tf_op jit(solution)/shard_map/while/body/eval_jaxpr/cond/branch_1_fun/jit(_take)/gather | solution.py:32
  294.2 9.5 %fusion.2 = f32[96,128,128]{2,1,0:T(8,128)S(1)} fusion(f32[96,128,128]{2,1,0:T(8,128)} %gather_fusion.1, f32[96,128,128]{2,1,0:T(8,128)} %gather_fusion, pred[96]{0:T(512)(128)(4,1)S(1)} %get-tuple-element.513, pred[96]{0:T(512)(128)(4,1)S(1)} %get-tuple-element.512), kind=kOutput, calls=%fused_computation.4 | convolution fusion | flops 2419064832 | bytes 18874560 | tf_op jit(solution)/shard_map/while/body/eval_jaxpr/cond/branch_1_fun/pik,pkj->pij/dot_general | solution.py:34
  303.8 6.3 %fusion.8 = f32[24,128,128]{2,0,1:T(8,128)S(1)} fusion(f32[24,128,128]{2,0,1:T(8,128)S(1)} %get-tuple-element.481, f32[96,128,128]{2,1,0:T(8,128)S(1)} %fusion.2, s32[96]{0:T(128)S(1)} %get-tuple-element.514, pred[96]{0:T(512)(128)(4,1)S(1)} %get-tuple-element.511), kind=kOutput, calls=%fused_computation.10 | convolution fusion | flops 453382656 | bytes 9437664 | tf_op jit(solution)/shard_map/while/body/eval_jaxpr/cond/branch_1_fun/op,pij->oij/dot_general | solution.py:39
  310.1 25.6 %conditional.2 = (f32[24,128,128]{2,0,1:T(8,128)S(1)}) conditional(s32[]{:T(128)} %convert_element_type.13, f32[24,128,128]{2,0,1:T(8,128)S(1)} %get-tuple-element.574, (s32[]{:T(128)}, s32[8,96,3]{1,2,0:T(4,128)S(1)}, s32[]{:T(128)}, f32[8,1,16,128,128]{4,3,2,1,0:T(8,128)}, f32[2,4,1,12,128,128]{5,4,3,2,1,0:T(8,128)}, ...), branch_computations={%region_1.1_spmd, %region_2.2_spmd} | conditional | flops 2872450304 | bytes 57163708 | solution.py:60
  311.4 3.5 %gather_fusion.1 = f32[96,128,128]{2,1,0:T(8,128)} fusion(f32[12,128,128]{2,1,0:T(8,128)S(1)} %dynamic-slice_bitcast_fusion.1, s32[1024]{0:T(1024)S(1)} %get-tuple-element.517), kind=kCustom, calls=%fused_computation.1 | custom fusion | bytes 12583296 | tf_op jit(solution)/shard_map/while/body/eval_jaxpr/cond/branch_1_fun/jit(_take)/gather | solution.py:33
  314.9 1.3 dynamic-slice_bitcast_fusion
  316.2 3.6 %gather_fusion = f32[96,128,128]{2,1,0:T(8,128)} fusion(f32[16,128,128]{2,1,0:T(8,128)S(1)} %dynamic-slice_bitcast_fusion, s32[1024]{0:T(1024)S(1)} %get-tuple-element.518), kind=kCustom, calls=%fused_computation | custom fusion | bytes 12583296 | tf_op jit(solution)/shard_map/while/body/eval_jaxpr/cond/branch_1_fun/jit(_take)/gather | solution.py:32
  319.8 9.5 %fusion.2 = f32[96,128,128]{2,1,0:T(8,128)S(1)} fusion(f32[96,128,128]{2,1,0:T(8,128)} %gather_fusion.1, f32[96,128,128]{2,1,0:T(8,128)} %gather_fusion, pred[96]{0:T(512)(128)(4,1)S(1)} %get-tuple-element.513, pred[96]{0:T(512)(128)(4,1)S(1)} %get-tuple-element.512), kind=kOutput, calls=%fused_computation.4 | convolution fusion | flops 2419064832 | bytes 18874560 | tf_op jit(solution)/shard_map/while/body/eval_jaxpr/cond/branch_1_fun/pik,pkj->pij/dot_general | solution.py:34
  329.4 6.3 %fusion.8 = f32[24,128,128]{2,0,1:T(8,128)S(1)} fusion(f32[24,128,128]{2,0,1:T(8,128)S(1)} %get-tuple-element.481, f32[96,128,128]{2,1,0:T(8,128)S(1)} %fusion.2, s32[96]{0:T(128)S(1)} %get-tuple-element.514, pred[96]{0:T(512)(128)(4,1)S(1)} %get-tuple-element.511), kind=kOutput, calls=%fused_computation.10 | convolution fusion | flops 453382656 | bytes 9437664 | tf_op jit(solution)/shard_map/while/body/eval_jaxpr/cond/branch_1_fun/op,pij->oij/dot_general | solution.py:39
  335.7 1.4 copy.13
  (76 shorter events, 16.3 us)
Async XLA Ops:
  6.5 116.9 %copy-start = (f32[1,1,16,128,128]{4,3,2,1,0:T(8,128)S(1)}, f32[1,1,16,128,128]{4,3,2,1,0:T(8,128)}, u32[]{:S(2)}) copy-start(f32[1,1,16,128,128]{4,3,2,1,0:T(8,128)} %param.7) | copy-start | bytes 3145732
  6.5 124.0 %all-gather.2.cloned.1.call-start = ((), (), s32[]{:S(2)}) async-start(), calls=%async_computation | async-start | bytes 7864320 | tf_op jit(solution)/shard_map/all_gather | solution.py:50
  6.5 16.1 %collective-permute-start = (f32[1,1,16,128,128]{4,3,2,1,0:T(8,128)}, f32[1,1,16,128,128]{4,3,2,1,0:T(8,128)S(1)}, u32[]{:S(2)}, u32[]{:S(2)}) collective-permute-start(f32[1,1,16,128,128]{4,3,2,1,0:T(8,128)} %param.7), channel_id=1, source_target_pairs={{0,4},{4,8},{8,12},{12,16},{16,20},{20,24},{24,28},{28,0},{1,5},{5... | collective-permute-start | bytes 3145736 | tf_op jit(solution)/shard_map/ppermute | solution.py:22
  22.7 15.1 %collective-permute-start.1 = (f32[1,1,16,128,128]{4,3,2,1,0:T(8,128)S(1)}, f32[1,1,16,128,128]{4,3,2,1,0:T(8,128)S(1)}, u32[]{:S(2)}, u32[]{:S(2)}) collective-permute-start(f32[1,1,16,128,128]{4,3,2,1,0:T(8,128)S(1)} %collective-permute-done), channel_id=1, source_target_pairs={{0,4},{4,8},{8,12},{12,16},{16,20},{20,24},{24,28},{28,0},{1,5},{5... | collective-permute-start | bytes 3145736 | tf_op jit(solution)/shard_map/ppermute | solution.py:22
  37.8 15.1 %collective-permute-start.2 = (f32[1,1,16,128,128]{4,3,2,1,0:T(8,128)S(1)}, f32[1,1,16,128,128]{4,3,2,1,0:T(8,128)S(1)}, u32[]{:S(2)}, u32[]{:S(2)}) collective-permute-start(f32[1,1,16,128,128]{4,3,2,1,0:T(8,128)S(1)} %collective-permute-done.1), channel_id=1, source_target_pairs={{0,4},{4,8},{8,12},{12,16},{16,20},{20,24},{24,28},{28,0},{1,5},{5... | collective-permute-start | bytes 3145736 | tf_op jit(solution)/shard_map/ppermute | solution.py:22
  52.9 1.0 copy-start.1
  53.9 15.1 %collective-permute-start.3 = (f32[1,1,16,128,128]{4,3,2,1,0:T(8,128)S(1)}, f32[1,1,16,128,128]{4,3,2,1,0:T(8,128)S(1)}, u32[]{:S(2)}, u32[]{:S(2)}) collective-permute-start(f32[1,1,16,128,128]{4,3,2,1,0:T(8,128)S(1)} %collective-permute-done.2), channel_id=1, source_target_pairs={{0,4},{4,8},{8,12},{12,16},{16,20},{20,24},{24,28},{28,0},{1,5},{5... | collective-permute-start | bytes 3145736 | tf_op jit(solution)/shard_map/ppermute | solution.py:22
  69.0 1.0 copy-start.3
  70.0 15.1 %collective-permute-start.4 = (f32[1,1,16,128,128]{4,3,2,1,0:T(8,128)S(1)}, f32[1,1,16,128,128]{4,3,2,1,0:T(8,128)S(1)}, u32[]{:S(2)}, u32[]{:S(2)}) collective-permute-start(f32[1,1,16,128,128]{4,3,2,1,0:T(8,128)S(1)} %collective-permute-done.3), channel_id=1, source_target_pairs={{0,4},{4,8},{8,12},{12,16},{16,20},{20,24},{24,28},{28,0},{1,5},{5... | collective-permute-start | bytes 3145736 | tf_op jit(solution)/shard_map/ppermute | solution.py:22
  85.1 1.0 copy-start.5
  86.1 15.2 %collective-permute-start.5 = (f32[1,1,16,128,128]{4,3,2,1,0:T(8,128)S(1)}, f32[1,1,16,128,128]{4,3,2,1,0:T(8,128)}, u32[]{:S(2)}, u32[]{:S(2)}) collective-permute-start(f32[1,1,16,128,128]{4,3,2,1,0:T(8,128)S(1)} %collective-permute-done.4), channel_id=1, source_target_pairs={{0,4},{4,8},{8,12},{12,16},{16,20},{20,24},{24,28},{28,0},{1,5},{5... | collective-permute-start | bytes 3145736 | tf_op jit(solution)/shard_map/ppermute | solution.py:22
  101.3 15.4 %collective-permute-start.6 = (f32[1,1,16,128,128]{4,3,2,1,0:T(8,128)}, f32[1,1,16,128,128]{4,3,2,1,0:T(8,128)}, u32[]{:S(2)}, u32[]{:S(2)}) collective-permute-start(f32[1,1,16,128,128]{4,3,2,1,0:T(8,128)} %collective-permute-done.5), channel_id=1, source_target_pairs={{0,4},{4,8},{8,12},{12,16},{16,20},{20,24},{24,28},{28,0},{1,5},{5... | collective-permute-start | bytes 3145736 | tf_op jit(solution)/shard_map/ppermute | solution.py:22
  102.0 24.1 %copy-start.6 = (f32[1,1,16,128,128]{4,3,2,1,0:T(8,128)S(1)}, f32[1,1,16,128,128]{4,3,2,1,0:T(8,128)}, u32[]{:S(2)}) copy-start(f32[1,1,16,128,128]{4,3,2,1,0:T(8,128)} %copy-done.5) | copy-start | bytes 3145732
  102.0 24.2 %copy-start.4 = (f32[1,1,16,128,128]{4,3,2,1,0:T(8,128)S(1)}, f32[1,1,16,128,128]{4,3,2,1,0:T(8,128)}, u32[]{:S(2)}) copy-start(f32[1,1,16,128,128]{4,3,2,1,0:T(8,128)} %copy-done.3) | copy-start | bytes 3145732
  102.1 24.3 %copy-start.2 = (f32[1,1,16,128,128]{4,3,2,1,0:T(8,128)S(1)}, f32[1,1,16,128,128]{4,3,2,1,0:T(8,128)}, u32[]{:S(2)}) copy-start(f32[1,1,16,128,128]{4,3,2,1,0:T(8,128)} %copy-done.1) | copy-start | bytes 3145732
Sparse Core Ops, SparseCore 0:
  8.9 118.0 all-gather.1
